TPU v7x, 32 devices: a whole 2x2x4 slice. The times are simulated.
32 devices in a mesh: frame: 8 (over z, x), head: 4 (over y, core).
Axes of the slice: x: 2, y: 2, z: 4, core: 2. Of those that a mesh axis runs over, the one named last changes fastest.
Arguments:
- tokens: bfloat16 [8, 576, 640], P('frame', 'head'), may hold values from -6 to 6
- ln_gain: float32 [2, 640], replicated, may hold values from 0.25 to 1.75
- qkv_weight: bfloat16 [2, 640, 1920], replicated, may hold values from -6 to 6
- out_weight: bfloat16 [2, 640, 640], replicated, may hold values from -0.3125 to 0.3125
Outputs:
- latents: bfloat16 [8, 576, 640], P('frame', 'head')
All inputs are finite; a program needn't handle non-finite values.
Results may differ from a plain program's by a relative error of at most 0.033.
The roundings to bfloat16 on the way count: a program that leaves them out, or rounds other values in their place, can miss the bound.
Values may be sent and summed in bfloat16 or wider, within the bound.
A program may use at most 64 MiB of HBM per device.

v0:
```python
import jax
import jax.numpy as jnp
from jax import lax
from jax.sharding import PartitionSpec as P

HEAD_DIM = 80
LAYERS = 2


def shifted(value, axis, steps):
    count = lax.axis_size(axis)
    initial, last = (max(0, -steps), min(count, count - steps))
    return lax.ppermute(value, axis, [(source, source + steps) for source in range(initial, last)])


def broadcast(value, axis, source):
    kept = jnp.where(lax.axis_index(axis) == source, value, 0).astype(value.dtype)
    return lax.psum(kept, axis)


def run_layer(state, gain, wqkv, wout, first_device):
    frames, rows, width = state.shape
    heads_dev = lax.axis_size("head")
    local = width // heads_dev
    xf = state.astype(jnp.float32)
    mean = jnp.mean(xf, axis=-1, keepdims=True)
    var = jnp.mean((xf - mean) ** 2, axis=-1, keepdims=True)
    normed = ((xf - mean) * lax.rsqrt(var + 1e-05) * gain).astype(jnp.bfloat16)
    offset = lax.axis_index("head") * local
    selected = lax.dynamic_slice_in_dim(wqkv.reshape(width, 3, width), offset, local, 2)
    qkv = jnp.einsum(
        "fnd,dce->fnce",
        lax.all_gather(normed, "head", axis=1, tiled=True),
        selected,
        preferred_element_type=jnp.float32,
    ).astype(jnp.bfloat16)
    pairs = qkv[:, :, 1:]
    boundary = shifted(pairs[-1], "frame", 1)
    pair_first = broadcast(pairs[0], "frame", 0)
    prev_own = jnp.where(first_device, pair_first, boundary)
    previous = jnp.concatenate([prev_own[None], pairs[:-1]], axis=0)
    head_size = HEAD_DIM
    heads_here = local // head_size
    scale = HEAD_DIM ** (-0.5)

    def attend(items):
        query, prev_pair = items
        count = query.shape[0]
        joined = jnp.concatenate([pair_first, prev_pair], axis=0)
        query_h = query.reshape(count, heads_here, head_size)
        keys = joined[:, 0].reshape(2 * count, heads_here, head_size)
        values = joined[:, 1].reshape(2 * count, heads_here, head_size)
        scores = (
            jnp.einsum("thd,shd->hts", query_h, keys, preferred_element_type=jnp.float32) * scale
        )
        top = jnp.max(scores, axis=-1, keepdims=True)
        expo = jnp.exp(scores - top)
        probs = (expo / jnp.sum(expo, axis=-1, keepdims=True)).astype(jnp.bfloat16)
        attended = jnp.einsum("hts,shd->thd", probs, values, preferred_element_type=jnp.float32)
        return attended.astype(jnp.bfloat16).reshape(count, local)

    attended = lax.map(attend, (qkv[:, :, 0], previous))
    returned = lax.all_to_all(attended, "head", split_axis=1, concat_axis=2, tiled=True)
    proj = jnp.dot(returned.reshape(frames * rows, width), wout, preferred_element_type=jnp.float32)
    return (xf + proj.reshape(frames, rows, width)).astype(jnp.bfloat16)


def shards(tokens, ln_gain, qkv_weight, out_weight):
    first_device = lax.axis_index("frame") == 0
    state = tokens
    for layer in range(LAYERS):
        state = run_layer(state, ln_gain[layer], qkv_weight[layer], out_weight[layer], first_device)
    return state


def solution(mesh):
    placed = (P("frame", "head", None), P(), P(), P())
    return jax.shard_map(
        shards, mesh=mesh, in_specs=placed, out_specs=P("frame", "head", None), check_vma=False
    )
```

profile of v0, /device:TPU:0, one launch (start us, length us, event | category | flops | bytes accessed | tf_op | source)
XLA Modules:
  0.0 246.2 jit_solution(362244257915139958)
XLA Ops:
  6.5 4.2 %fusion.38 = (bf16[1,640,1920]{2,1,0:T(8,128)(2,1)S(1)}, bf16[1,640,1920]{2,1,0:T(8,128)(2,1)}) fusion(bf16[2,640,1920]{2,1,0:T(8,128)(2,1)} %param.6), kind=kLoop, calls=%fused_computation.70 | loop fusion | bytes 9830400 | tf_op jit(solution)/shard_map/slice | solution.py:72
  10.8 4.4 %copy.11 = bf16[1,640,1920]{1,2,0:T(8,128)(2,1)} copy(bf16[1,640,1920]{2,1,0:T(8,128)(2,1)} %get-tuple-element.31) | data formatting | bytes 4915200 | tf_op jit(solution)/shard_map/slice | solution.py:72
  15.7 9.8 %all_gather.6 = bf16[1,576,640]{2,1,0:T(8,128)(2,1)S(1)} all-gather(bf16[1,144,640]{2,1,0:T(8,128)(2,1)S(1)} %fusion.25), channel_id=1, replica_groups=mesh['frame'=8,'head'=4] {'head'}, dimensions={1}, use_global_device_ids=true | all-gather | bytes 921600 | tf_op jit(solution)/shard_map/all_gather | solution.py:33
  29.0 4.2 %collective-permute-start = (bf16[576,2,160]{0,2,1:T(8,128)(2,1)}, bf16[576,2,160]{0,2,1:T(8,128)(2,1)}, u32[]{:S(2)}, u32[]{:S(2)}) collective-permute-start(bf16[576,2,160]{0,2,1:T(8,128)(2,1)} %slice_bitcast_fusion.1), channel_id=1, source_target_pairs={{0,4},{4,8},{8,12},{12,16},{16,20},{20,24},{24,28},{1,5},{5,9},{9,... | collective-permute-start | bytes 1105928 | tf_op jit(solution)/shard_map/ppermute | solution.py:13
  33.9 68.9 %all-reduce.3.cloned.1.call-done = bf16[576,2,160]{0,2,1:T(8,128)(2,1)} async-done(((bf16[576,2,160]{0,2,1:T(8,128)(2,1)}), bf16[576,2,160]{0,2,1:T(8,128)(2,1)}) %all-reduce.3.cloned.1.call-update) | async-done | bytes 368656 | tf_op jit(solution)/shard_map/psum | solution.py:18
  103.8 2.1 pad_maximum_fusion.1
  105.9 3.1 %exponential_reduce_fusion.1 = f32[2,576]{1,0:T(2,128)S(1)} fusion(bf16[576,2,80]{0,2,1:T(8,128)(2,1)} %bitcast.102, bf16[1152,2,80]{0,2,1:T(8,128)(2,1)} %bitcast.94), kind=kOutput, calls=%fused_computation.9 | convolution fusion | flops 216319104 | bytes 557568 | tf_op jit(solution)/shard_map/while/body/eval_jaxpr/sub | solution.py:57
  109.0 4.2 %fusion.7 = bf16[2,80,576]{2,1,0:T(8,128)(2,1)} fusion(bf16[1152,2,80]{0,2,1:T(8,128)(2,1)S(1)} %bitcast.96, f32[2,576]{1,0:T(2,128)S(1)} %exponential_reduce_fusion.1, bf16[576,2,80]{0,2,1:T(8,128)(2,1)} %bitcast.103, bf16[1152,2,80]{0,2,1:T(8,128)(2,1)S(1)} %bitcast.95), kind=kOutput, calls=%fused_computation.15 | convolution fusion | flops 430076160 | bytes 1110528 | tf_op jit(solution)/shard_map/while/body/eval_jaxpr/hts,shd->thd/dot_general | solution.py:59
  113.2 1.7 copy.12
  115.5 3.2 %reduce.8 = bf16[576,160]{1,0:T(8,128)(2,1)} reduce(bf16[576,1,160]{2,1,0:T(2,128)(2,1)S(1)} %bitcast.88, bf16[]{:T(256)} %broadcast.90), dimensions={1}, to_apply=%bitcast.62.reduce_sub_computation | reduce | bytes 368642
  118.7 2.0 reshape.114
  120.7 3.4 %all-to-all-start = ((bf16[4,2,11520]{2,1,0:T(2,128)(2,1)}), bf16[4,2,11520]{2,1,0:T(2,128)(2,1)S(1)}, u32[]{:S(2)}, u32[]{:S(2)}) async-start(bf16[4,2,11520]{2,1,0:T(2,128)(2,1)} %reshape.114), calls=%async_computation | async-start | bytes 368640 | tf_op jit(solution)/shard_map/all_to_all | solution.py:63
  124.3 2.6 %copy.15 = bf16[1,640,1920]{1,2,0:T(8,128)(2,1)} copy(bf16[1,640,1920]{2,1,0:T(8,128)(2,1)S(1)} %get-tuple-element.30) | data formatting | bytes 4915200 | tf_op jit(solution)/shard_map/slice | solution.py:72
  128.1 1.2 all-to-all-done
  131.4 1.6 fusion.39
  133.4 7.7 %all_gather.7 = bf16[1,576,640]{2,1,0:T(8,128)(2,1)S(1)} all-gather(bf16[1,144,640]{2,1,0:T(8,128)(2,1)S(1)} %multiply_convert_fusion), channel_id=1, replica_groups=mesh['frame'=8,'head'=4] {'head'}, dimensions={1}, use_global_device_ids=true | all-gather | bytes 921600 | tf_op jit(solution)/shard_map/all_gather | solution.py:33
  142.8 2.6 %collective-permute-start.1 = (bf16[576,2,160]{0,2,1:T(8,128)(2,1)S(1)}, bf16[576,2,160]{0,2,1:T(8,128)(2,1)S(1)}, u32[]{:S(2)}, u32[]{:S(2)}) collective-permute-start(bf16[576,2,160]{0,2,1:T(8,128)(2,1)S(1)} %slice_bitcast_fusion), channel_id=1, source_target_pairs={{0,4},{4,8},{8,12},{12,16},{16,20},{20,24},{24,28},{1,5},{5,9},{9,... | collective-permute-start | bytes 1105928 | tf_op jit(solution)/shard_map/ppermute | solution.py:13
  145.4 10.5 %collective-permute-done.1 = bf16[576,2,160]{0,2,1:T(8,128)(2,1)S(1)} collective-permute-done((bf16[576,2,160]{0,2,1:T(8,128)(2,1)S(1)}, bf16[576,2,160]{0,2,1:T(8,128)(2,1)S(1)}, u32[]{:S(2)}, u32[]{:S(2)}) %collective-permute-start.1) | collective-permute-done | bytes 368672 | tf_op jit(solution)/shard_map/ppermute | solution.py:13
  155.9 61.8 %all-reduce.5.cloned.1.call-done = bf16[576,2,160]{0,2,1:T(8,128)(2,1)} async-done(((bf16[576,2,160]{0,2,1:T(8,128)(2,1)}), bf16[576,2,160]{0,2,1:T(8,128)(2,1)}) %all-reduce.5.cloned.1.call-update) | async-done | bytes 368656 | tf_op jit(solution)/shard_map/psum | solution.py:18
  218.8 1.2 pad_maximum_fusion
  220.0 1.9 exponential_reduce_fusion
  221.9 2.6 %fusion.6 = bf16[2,80,576]{2,1,0:T(8,128)(2,1)S(1)} fusion(bf16[1152,2,80]{0,2,1:T(8,128)(2,1)S(1)} %bitcast.99, f32[2,576]{1,0:T(2,128)S(1)} %exponential_reduce_fusion, bf16[576,2,80]{0,2,1:T(8,128)(2,1)S(1)} %bitcast.101, bf16[1152,2,80]{0,2,1:T(8,128)(2,1)S(1)} %bitcast.98), kind=kOutput, calls=%fused_computation.14 | convolution fusion | flops 430076160 | bytes 1110528 | tf_op jit(solution)/shard_map/while/body/eval_jaxpr/hts,shd->thd/dot_general | solution.py:59
  225.4 2.6 %reduce.9 = bf16[576,160]{1,0:T(8,128)(2,1)S(1)} reduce(bf16[576,1,160]{2,1,0:T(2,128)(2,1)S(1)} %bitcast.89, bf16[]{:T(256)} %broadcast.90), dimensions={1}, to_apply=%bitcast.64.reduce_sub_computation | reduce | bytes 368642
  228.5 7.7 %all_to_all.30 = bf16[4,2,11520]{2,1,0:T(2,128)(2,1)S(1)} all-to-all(bf16[4,2,11520]{2,1,0:T(2,128)(2,1)S(1)} %reshape.116), channel_id=1, replica_groups=mesh['frame'=8,'head'=4] {'head'}, dimensions={0} | all-to-all | bytes 368640 | tf_op jit(solution)/shard_map/all_to_all | solution.py:63
  (53 shorter events, 17.3 us)
Async XLA Ops:
  6.5 96.2 %all-reduce.3.cloned.1.call-start = ((), (), s32[]{:S(2)}) async-start(), calls=%async_computation.2 | async-start | bytes 819200 | tf_op jit(solution)/shard_map/psum | solution.py:18
  10.8 4.4 %copy-start.4 = (f32[2,640]{1,0:T(2,128)S(1)}, f32[2,640]{1,0:T(2,128)}, u32[]{:S(2)}) copy-start(f32[2,640]{1,0:T(2,128)} %param.5) | copy-start | bytes 15364
  10.8 4.4 %copy-start = (bf16[1,144,640]{2,1,0:T(8,128)(2,1)S(1)}, bf16[1,144,640]{2,1,0:T(8,128)(2,1)}, u32[]{:S(2)}) copy-start(bf16[1,144,640]{2,1,0:T(8,128)(2,1)} %param.4) | copy-start | bytes 552964
  29.0 73.8 %collective-permute-start = (bf16[576,2,160]{0,2,1:T(8,128)(2,1)}, bf16[576,2,160]{0,2,1:T(8,128)(2,1)}, u32[]{:S(2)}, u32[]{:S(2)}) collective-permute-start(bf16[576,2,160]{0,2,1:T(8,128)(2,1)} %slice_bitcast_fusion.1), channel_id=1, source_target_pairs={{0,4},{4,8},{8,12},{12,16},{16,20},{20,24},{24,28},{1,5},{5,9},{9,... | collective-permute-start | bytes 1105928 | tf_op jit(solution)/shard_map/ppermute | solution.py:13
  105.9 3.1 %copy-start.2 = (bf16[1152,1,160]{0,2,1:T(8,128)(2,1)S(1)}, bf16[1152,1,160]{0,2,1:T(8,128)(2,1)}, u32[]{:S(2)}) copy-start(bf16[1152,1,160]{0,2,1:T(8,128)(2,1)} %get-tuple-element.34) | copy-start | bytes 1105924
  105.9 3.1 %copy-start.3 = (bf16[1152,1,160]{0,2,1:T(8,128)(2,1)S(1)}, bf16[1152,1,160]{0,2,1:T(8,128)(2,1)}, u32[]{:S(2)}) copy-start(bf16[1152,1,160]{0,2,1:T(8,128)(2,1)} %get-tuple-element.40) | copy-start | bytes 1105924
  120.7 8.5 %all-to-all-start = ((bf16[4,2,11520]{2,1,0:T(2,128)(2,1)}), bf16[4,2,11520]{2,1,0:T(2,128)(2,1)S(1)}, u32[]{:S(2)}, u32[]{:S(2)}) async-start(bf16[4,2,11520]{2,1,0:T(2,128)(2,1)} %reshape.114), calls=%async_computation | async-start | bytes 368640 | tf_op jit(solution)/shard_map/all_to_all | solution.py:63
  124.1 93.6 %all-reduce.5.cloned.1.call-start = ((), (), s32[]{:S(2)}) async-start(), calls=%async_computation.3 | async-start | bytes 819200 | tf_op jit(solution)/shard_map/psum | solution.py:18
  142.8 13.2 %collective-permute-start.1 = (bf16[576,2,160]{0,2,1:T(8,128)(2,1)S(1)}, bf16[576,2,160]{0,2,1:T(8,128)(2,1)S(1)}, u32[]{:S(2)}, u32[]{:S(2)}) collective-permute-start(bf16[576,2,160]{0,2,1:T(8,128)(2,1)S(1)} %slice_bitcast_fusion), channel_id=1, source_target_pairs={{0,4},{4,8},{8,12},{12,16},{16,20},{20,24},{24,28},{1,5},{5,9},{9,... | collective-permute-start | bytes 1105928 | tf_op jit(solution)/shard_map/ppermute | solution.py:13
  224.5 13.9 %copy-start.1 = (bf16[2,640,640]{2,1,0:T(8,128)(2,1)S(1)}, bf16[2,640,640]{2,1,0:T(8,128)(2,1)}, u32[]{:S(2)}) copy-start(bf16[2,640,640]{2,1,0:T(8,128)(2,1)} %param.7) | copy-start | bytes 4915204
Sparse Core Ops, SparseCore 0:
  28.3 74.3 all-reduce.2
  145.5 72.1 all-reduce.4
where the time goes:
time: 247 us; the launch traced here: 246 us
  waiting for transfers between devices  142 us (57%)
  blocking collectives  25.3 us (10%)
  local copies, waits for them, and re-layouts  24.9 us (10%)
  matrix products  15.7 us (6%)
  other arithmetic  13.8 us (6%)
  between operations  13.7 us (6%)
  starting transfers between devices  10.4 us (4%)
    psum x2, waiting for transfers between devices, broadcast(): return lax.psum(kept, axis)  131 us
    all_gather x2, blocking collectives, run_layer(): lax.all_gather(normed, 'head', axis=1, tiled=True)  17.5 us
    slice x3, local copies, waits for them, and re-layouts, shards(): qkv_weight[layer]  11.2 us
    ppermute x2, waiting for transfers between devices, shifted(): lax.ppermute(value, axis, [(source, source + steps) for source in range(i...  10.5 us
    all_to_all x1, blocking collectives, run_layer(): lax.all_to_all(attended, 'head', split_axis=1, concat_axis=2, tiled=True)  7.74 us
    ppermute x2, starting transfers between devices, shifted(): lax.ppermute(value, axis, [(source, source + steps) for source in range(i...  6.78 us
    dot_general x2, matrix products, attend(): jnp.einsum('hts,shd->thd', probs, values, preferred_element_type=jnp.floa...  6.73 us
    unnamed x2, other arithmetic  5.82 us
  transfers between devices with their start and end apart: 5, of which 4 were waited for; matrix products, arithmetic and copies ran while one was open for 2% of the time, Pallas kernels for 0%

commit v1 on v0

v1 whole, which is shorter than its diff:
```python
import functools
import math
import jax
import jax.numpy as jnp
from jax import lax
from jax.experimental import pallas as pl
from jax.experimental.pallas import tpu as pltpu
from jax.sharding import PartitionSpec as P

HEADS = 8
HEAD_DIM = 80
PAD = 128
LAYERS = 2
CHUNKS = 3
SCALE2 = HEAD_DIM ** (-0.5) * math.log2(math.e)
MESH = pl.DeviceIdType.MESH
CHILD, MATE, ACROSS, RELAY, EXTRA = range(5)


def kernel(nf, tok, gain, wqkv_hbm, wout_hbm, out, wraw, wpad, wo, nb, own, xs, q, kv, att,
           wsem, osem, ssem, rsem):
    f = lax.axis_index("frame")
    h = lax.axis_index("head")
    rows, width = own.shape[1:]
    step = rows // CHUNKS
    mate = h + 1 - 2 * (h % 2)
    across = (h + 2) % 4
    diag = (mate + 2) % 4

    barrier = pltpu.get_barrier_semaphore()
    for hh in (mate, across):
        pl.semaphore_signal(barrier, inc=1, device_id=(f, hh), device_id_type=MESH)
    for d in (-2, -1, 1, 2):
        @pl.when((f + d >= 0) & (f + d < nf))
        def _():
            pl.semaphore_signal(barrier, inc=1, device_id=(f + d, h), device_id_type=MESH)

    def weight_copy(l):
        return pltpu.make_async_copy(wqkv_hbm.at[l], wraw.at[l], wsem.at[l])

    def wout_copy(l, j):
        return pltpu.make_async_copy(wout_hbm.at[l, pl.ds(j * HEAD_DIM, HEAD_DIM)],
                                     wo.at[l, pl.ds(j * PAD, HEAD_DIM)], osem.at[l, j])

    for l in range(LAYERS):
        weight_copy(l).start()
        for j in range(HEADS):
            wout_copy(l, j).start()

    def norm(l, xf):
        mean = jnp.mean(xf, axis=-1, keepdims=True)
        cen = xf - mean
        var = jnp.mean(cen * cen, axis=-1, keepdims=True)
        n = (cen * lax.rsqrt(var + 1e-05) * gain[l:l + 1, :]).astype(jnp.bfloat16)
        own[l] = n

        @pl.when(f == 0)
        def _():
            nb[l, 0, h] = n

    def copy(src, l, kind, quarter, c, who, dev):
        return pltpu.make_async_remote_copy(
            src_ref=src, dst_ref=nb.at[l, kind, quarter, pl.ds(c * step, step)],
            send_sem=ssem.at[l, kind, who, c], recv_sem=rsem.at[l, kind, quarter, c],
            device_id=dev, device_id_type=MESH)

    def part(l, kind, quarter, c):
        return nb.at[l, kind, quarter, pl.ds(c * step, step)]

    def landed(l, kind, quarter, c):
        copy(part(l, kind, quarter, c), l, kind, quarter, c, MATE, (f, mate)).wait_recv()

    def spread(l, kind, c):
        src = part(l, kind, h, c)
        copy(src, l, kind, h, c, ACROSS, (f, across)).start()
        copy(src, l, kind, h, c, MATE, (f, mate)).start()

    def first_step(l, c):
        @pl.when(f > 0)
        def _():
            landed(l, 0, h, c)
        src = part(l, 0, h, c)

        @pl.when(f + 2 < nf)
        def _():
            copy(src, l, 0, h, c, CHILD, (f + 2, h)).start()

        @pl.when(f == 0)
        def _():
            copy(src, l, 0, h, c, EXTRA, (f + 1, h)).start()
        spread(l, 0, c)

    def send_prev(l):
        @pl.when((f > 0) & (f + 1 < nf))
        def _():
            for c in range(CHUNKS):
                copy(own.at[l, pl.ds(c * step, step)], l, 1, h, c, CHILD, (f + 1, h)).start()

    def prev_step(l, c):
        landed(l, 1, h, c)
        spread(l, 1, c)

    def relay(l, kind):
        for c in range(CHUNKS):
            landed(l, kind, across, c)
            copy(part(l, kind, across, c), l, kind, across, c, RELAY, (f, mate)).start()

    def mate_landed(l, kind):
        for quarter in (mate, diag):
            for c in range(CHUNKS):
                landed(l, kind, quarter, c)

    def drain(l):
        def one(kind, who, dev):
            for c in range(CHUNKS):
                copy(part(l, kind, h, c), l, kind, h, c, who, dev).wait_send()

        def group(kind):
            one(kind, MATE, (f, mate))
            one(kind, ACROSS, (f, across))
            one(kind, RELAY, (f, mate))
        group(0)

        @pl.when(f >= 2)
        def _():
            group(1)

        @pl.when(f + 2 < nf)
        def _():
            one(0, CHILD, (f + 2, h))

        @pl.when(f == 0)
        def _():
            one(0, EXTRA, (f + 1, h))

        @pl.when((f > 0) & (f + 1 < nf))
        def _():
            one(1, CHILD, (f + 1, h))

    def widen(l):
        weight_copy(l).wait()

        @pl.loop(0, width // 64)
        def _(i):
            r = pl.ds(pl.multiple_of(i * 64, 64), 64)
            w = wraw[l, r, :]
            zero = jnp.zeros((64, PAD - HEAD_DIM), jnp.bfloat16)
            for j in range(3 * HEADS):
                wpad[l, r, j * PAD:j * PAD + PAD] = jnp.concatenate(
                    [w[:, j * HEAD_DIM:(j + 1) * HEAD_DIM], zero], axis=1)
        for j in range(HEADS):
            wo[l, j * PAD + HEAD_DIM:(j + 1) * PAD, :] = jnp.zeros((PAD - HEAD_DIM, width), jnp.bfloat16)
            wout_copy(l, j).wait()

    def query(l):
        @pl.loop(0, HEADS * PAD // 256)
        def _(i):
            cols = pl.ds(pl.multiple_of(i * 256, 256), 256)
            q[:, cols] = jnp.dot(own[l], wpad[l, :, cols],
                                 preferred_element_type=jnp.float32).astype(jnp.bfloat16)

    def keys_values(l, kind):
        count = 4 * rows

        @pl.loop(0, 2 * HEADS * PAD // 256)
        def _(i):
            cols = pl.ds(pl.multiple_of(i * 256, 256), 256)
            wcols = pl.ds(pl.multiple_of(HEADS * PAD + i * 256, 256), 256)
            n = nb[l, kind].reshape(count, width)
            kv[kind * count:(kind + 1) * count, cols] = jnp.dot(
                n, wpad[l, :, wcols], preferred_element_type=jnp.float32).astype(jnp.bfloat16)

    def attend(count, hook):
        @pl.loop(0, HEADS // 2)
        def _(i):
            if hook is not None:
                @pl.when(i == HEADS // 2 - 1)
                def _():
                    hook()
            for j in range(2):
                cols = pl.ds(pl.multiple_of(i * (2 * PAD) + j * PAD, PAD), PAD)
                vcols = pl.ds(pl.multiple_of(HEADS * PAD + i * (2 * PAD) + j * PAD, PAD), PAD)
                s = lax.dot_general(q[:, cols], kv[:count, cols], (((1,), (1,)), ((), ())),
                                    preferred_element_type=jnp.float32)
                top = jnp.max(s, axis=-1, keepdims=True)
                e = jnp.exp2((s - top) * SCALE2)
                p = (e * (1.0 / jnp.sum(e, axis=-1, keepdims=True))).astype(jnp.bfloat16)
                att[:, cols] = jnp.dot(p, kv[:count, vcols],
                                       preferred_element_type=jnp.float32).astype(jnp.bfloat16)

    def first_steps(l):
        for c in range(CHUNKS):
            first_step(l, c)

    xf = tok[0].astype(jnp.float32)
    norm(0, xf)
    xs[...] = xf
    near = 2 + ((f > 0).astype(jnp.int32) + (f > 1).astype(jnp.int32)
                + (f < nf - 1).astype(jnp.int32) + (f < nf - 2).astype(jnp.int32))
    pl.semaphore_wait(barrier, near)

    for l in range(LAYERS):
        send_prev(l)
        if l == 0:
            @pl.when(f == 0)
            def _():
                first_steps(0)
            widen(0)
            query(0)

            @pl.when((f == 1))
            def _():
                first_steps(0)

            @pl.when((f == 2) | (f == 3))
            def _():
                for c in range(CHUNKS):
                    first_step(0, c)
                    prev_step(0, c)

            @pl.when(f >= 4)
            def _():
                for c in range(CHUNKS):
                    prev_step(0, c)
                first_steps(0)

            @pl.when(f >= 2)
            def _():
                relay(0, 1)
            relay(0, 0)

            @pl.when(f >= 2)
            def _():
                mate_landed(0, 1)
                keys_values(0, 1)
            mate_landed(0, 0)
            keys_values(0, 0)
        else:
            @pl.when(f == 0)
            def _():
                first_steps(l)
            query(l)
            relay(l, 0)
            mate_landed(l, 0)
            keys_values(l, 0)

            @pl.when(f >= 2)
            def _():
                for c in range(CHUNKS):
                    prev_step(l, c)
                relay(l, 1)
                mate_landed(l, 1)
                keys_values(l, 1)

        def ahead():
            @pl.when(f > 0)
            def _():
                first_steps(l + 1)

        hook = ahead if l + 1 < LAYERS else None
        if l == 0:
            widen(1)

        @pl.when(f < 2)
        def _():
            attend(4 * rows, hook)

        @pl.when(f >= 2)
        def _():
            attend(8 * rows, hook)

        proj = jnp.dot(att[...], wo[l], preferred_element_type=jnp.float32)
        x = (xs[...] + proj).astype(jnp.bfloat16)
        if l + 1 < LAYERS:
            xf = x.astype(jnp.float32)
            xs[...] = xf
            norm(l + 1, xf)
        else:
            out[0] = x
    for l in range(LAYERS):
        drain(l)


def shards(nf, tokens, ln_gain, qkv_weight, out_weight):
    _, rows, width = tokens.shape
    bf = jnp.bfloat16
    vmem = pl.BlockSpec(memory_space=pltpu.VMEM)
    hbm = pl.BlockSpec(memory_space=pl.ANY)
    return pl.pallas_call(
        functools.partial(kernel, nf),
        out_shape=jax.ShapeDtypeStruct(tokens.shape, bf),
        in_specs=[vmem, vmem, hbm, hbm],
        out_specs=vmem,
        scratch_shapes=[
            pltpu.VMEM((LAYERS, width, 3 * width), bf),
            pltpu.VMEM((LAYERS, width, 3 * HEADS * PAD), bf),
            pltpu.VMEM((LAYERS, HEADS * PAD, width), bf),
            pltpu.VMEM((LAYERS, 2, 4, rows, width), bf),
            pltpu.VMEM((LAYERS, rows, width), bf),
            pltpu.VMEM((rows, width), jnp.float32),
            pltpu.VMEM((rows, HEADS * PAD), bf),
            pltpu.VMEM((8 * rows, 2 * HEADS * PAD), bf),
            pltpu.VMEM((rows, HEADS * PAD), bf),
            pltpu.SemaphoreType.DMA((LAYERS,)),
            pltpu.SemaphoreType.DMA((LAYERS, HEADS)),
            pltpu.SemaphoreType.DMA((LAYERS, 2, 5, CHUNKS)),
            pltpu.SemaphoreType.DMA((LAYERS, 2, 4, CHUNKS)),
        ],
        compiler_params=pltpu.CompilerParams(
            collective_id=0, has_side_effects=True, vmem_limit_bytes=56 * 1024 * 1024),
    )(tokens, ln_gain, qkv_weight, out_weight)


def solution(mesh):
    placed = (P("frame", "head", None), P(), P(), P())
    return jax.shard_map(
        functools.partial(shards, mesh.shape["frame"]), mesh=mesh, in_specs=placed,
        out_specs=P("frame", "head", None), check_vma=False
    )
```

time: 247 us -> 66.8 us (0.27)
  the two profiles are of different devices: /device:TPU:0 before, /device:TPU:27 now
where the time goes in v1:
time: 66.8 us; the launch traced here: 66.6 us
  Pallas kernels  65 us (97%)
  local copies, waits for them, and re-layouts  1.61 us (2%)
    pallas_call x1, Pallas kernels, shards(): pl.pallas_call(functools.partial(kernel, nf), out_shape=jax.ShapeDtypeStr...  65 us
    unnamed x1, local copies, waits for them, and re-layouts  1.61 us

profile of v1, /device:TPU:27, one launch (start us, length us, event | category | flops | bytes accessed | tf_op | source)
XLA Modules:
  0.0 66.6 jit_solution(5095906044319946641)
XLA Ops:
  0.0 65.0 %shard_map.46 = bf16[1,144,640]{2,1,0:T(8,128)(2,1)} custom-call(bf16[1,144,640]{2,1,0:T(8,128)(2,1)} %tok.1, f32[2,640]{1,0:T(2,128)} %gain.1, bf16[2,640,1920]{2,1,0:T(8,128)(2,1)} %wqkv_hbm.1, bf16[2,640,640]{2,1,0:T(8,128)(2,1)} %wout_hbm.1), custom_call_target="tpu_custom_call" | custom-call | tf_op jit(solution)/shard_map/pallas_call | solution.py:289
  65.0 1.6 %copy.6 = bf16[1,144,640]{2,1,0:T(8,128)(2,1)} copy(bf16[1,144,640]{2,1,0:T(8,128)(2,1)} %shard_map.46) | data formatting | bytes 368640

commit v2 on v1

--- a/solution.py
+++ b/solution.py
@@ -12,12 +12,13 @@
 PAD = 128
 LAYERS = 2
 CHUNKS = 3
+GROUP = 4
 SCALE2 = HEAD_DIM ** (-0.5) * math.log2(math.e)
 MESH = pl.DeviceIdType.MESH
 CHILD, MATE, ACROSS, RELAY, EXTRA = range(5)
 
 
-def kernel(nf, tok, gain, wqkv_hbm, wout_hbm, out, wraw, wpad, wo, nb, own, xs, q, kv, att,
+def kernel(nf, tok, gain, wqkv_hbm, wout_hbm, out, wraw, wpad, wo, nb, own, xs, q, kv, att, acc, top_ref, sum_ref,
            wsem, osem, ssem, rsem):
     f = lax.axis_index("frame")
     h = lax.axis_index("head")
@@ -159,38 +160,92 @@
             q[:, cols] = jnp.dot(own[l], wpad[l, :, cols],
                                  preferred_element_type=jnp.float32).astype(jnp.bfloat16)
 
-    def keys_values(l, kind):
-        count = 4 * rows
-
-        @pl.loop(0, 2 * HEADS * PAD // 256)
-        def _(i):
-            cols = pl.ds(pl.multiple_of(i * 256, 256), 256)
-            wcols = pl.ds(pl.multiple_of(HEADS * PAD + i * 256, 256), 256)
-            n = nb[l, kind].reshape(count, width)
-            kv[kind * count:(kind + 1) * count, cols] = jnp.dot(
-                n, wpad[l, :, wcols], preferred_element_type=jnp.float32).astype(jnp.bfloat16)
-
-    def attend(count, hook):
-        @pl.loop(0, HEADS // 2)
+    half = 4 * rows
+    heads_cols = HEADS * PAD
+
+    def keys_values(l, kind, between=None):
+        n = nb[l, kind].reshape(half, width)
+        for j in range(2):
+            if between is not None:
+                between[j]()
+            kv[kind * half:(kind + 1) * half, j * heads_cols:(j + 1) * heads_cols] = jnp.dot(
+                n, wpad[l, :, (j + 1) * heads_cols:(j + 2) * heads_cols],
+                preferred_element_type=jnp.float32).astype(jnp.bfloat16)
+
+    def attend(kind, stage, hook=None):
+        @pl.loop(0, HEADS // GROUP)
         def _(i):
             if hook is not None:
-                @pl.when(i == HEADS // 2 - 1)
+                @pl.when(i == HEADS // GROUP - 1)
                 def _():
                     hook()
-            for j in range(2):
-                cols = pl.ds(pl.multiple_of(i * (2 * PAD) + j * PAD, PAD), PAD)
-                vcols = pl.ds(pl.multiple_of(HEADS * PAD + i * (2 * PAD) + j * PAD, PAD), PAD)
-                s = lax.dot_general(q[:, cols], kv[:count, cols], (((1,), (1,)), ((), ())),
+            keys = slice(kind * half, (kind + 1) * half)
+            for j in range(GROUP):
+                cols = pl.ds(pl.multiple_of((i * GROUP + j) * PAD, PAD), PAD)
+                vcols = pl.ds(pl.multiple_of(heads_cols + (i * GROUP + j) * PAD, PAD), PAD)
+                head = i * GROUP + j
+                s = lax.dot_general(q[:, cols], kv[keys, cols], (((1,), (1,)), ((), ())),
                                     preferred_element_type=jnp.float32)
                 top = jnp.max(s, axis=-1, keepdims=True)
+                if stage == "last":
+                    before = top_ref[head]
+                    top = jnp.maximum(top, before)
                 e = jnp.exp2((s - top) * SCALE2)
-                p = (e * (1.0 / jnp.sum(e, axis=-1, keepdims=True))).astype(jnp.bfloat16)
-                att[:, cols] = jnp.dot(p, kv[:count, vcols],
-                                       preferred_element_type=jnp.float32).astype(jnp.bfloat16)
+                total = jnp.sum(e, axis=-1, keepdims=True)
+                part_out = jnp.dot(e.astype(jnp.bfloat16), kv[keys, vcols],
+                                   preferred_element_type=jnp.float32)
+                if stage == "first":
+                    top_ref[head] = top
+                    sum_ref[head] = total
+                    acc[:, cols] = part_out
+                    continue
+                if stage == "last":
+                    fade = jnp.exp2((before - top) * SCALE2)
+                    total = total + sum_ref[head] * fade
+                    part_out = part_out + acc[:, cols] * fade
+                att[:, cols] = (part_out * (1.0 / total)).astype(jnp.bfloat16)
 
     def first_steps(l):
         for c in range(CHUNKS):
             first_step(l, c)
+
+    def prev_steps(l):
+        for c in range(CHUNKS):
+            prev_step(l, c)
+
+    def both_steps(l):
+        for c in range(CHUNKS):
+            first_step(l, c)
+            prev_step(l, c)
+
+    def two_halves_first(l):
+        relay(l, 1)
+        mate_landed(l, 1)
+        keys_values(l, 1)
+        attend(1, "first", functools.partial(relay, l, 0))
+        mate_landed(l, 0)
+        keys_values(l, 0)
+
+        @pl.when(f + 2 < nf)
+        def _():
+            first_steps(l + 1)
+        attend(0, "last")
+
+    def two_halves_second(l):
+        relay(l, 0)
+        mate_landed(l, 0)
+        keys_values(l, 0, [functools.partial(prev_step, l, c) for c in range(2)])
+        prev_step(l, 2)
+        attend(0, "first", functools.partial(relay, l, 1))
+        mate_landed(l, 1)
+        keys_values(l, 1)
+        attend(1, "last")
+
+    def one_half(l):
+        relay(l, 0)
+        mate_landed(l, 0)
+        keys_values(l, 0)
+        attend(0, "only")
 
     xf = tok[0].astype(jnp.float32)
     norm(0, xf)
@@ -201,73 +256,50 @@
 
     for l in range(LAYERS):
         send_prev(l)
+
         if l == 0:
             @pl.when(f == 0)
             def _():
-                first_steps(0)
+                first_steps(l)
             widen(0)
-            query(0)
-
-            @pl.when((f == 1))
-            def _():
-                first_steps(0)
+        else:
+            @pl.when((f < 2) | (f + 2 >= nf))
+            def _():
+                first_steps(l)
+        query(l)
+        if l == 0:
+            @pl.when((f == 0) | (f >= 4))
+            def _():
+                widen(1)
+
+        if l == 0:
+            @pl.when(f == 1)
+            def _():
+                first_steps(l)
 
             @pl.when((f == 2) | (f == 3))
             def _():
-                for c in range(CHUNKS):
-                    first_step(0, c)
-                    prev_step(0, c)
+                both_steps(l)
 
             @pl.when(f >= 4)
             def _():
-                for c in range(CHUNKS):
-                    prev_step(0, c)
-                first_steps(0)
-
-            @pl.when(f >= 2)
-            def _():
-                relay(0, 1)
-            relay(0, 0)
-
-            @pl.when(f >= 2)
-            def _():
-                mate_landed(0, 1)
-                keys_values(0, 1)
-            mate_landed(0, 0)
-            keys_values(0, 0)
-        else:
-            @pl.when(f == 0)
-            def _():
+                prev_steps(l)
                 first_steps(l)
-            query(l)
-            relay(l, 0)
-            mate_landed(l, 0)
-            keys_values(l, 0)
-
-            @pl.when(f >= 2)
-            def _():
-                for c in range(CHUNKS):
-                    prev_step(l, c)
-                relay(l, 1)
-                mate_landed(l, 1)
-                keys_values(l, 1)
-
-        def ahead():
-            @pl.when(f > 0)
-            def _():
-                first_steps(l + 1)
-
-        hook = ahead if l + 1 < LAYERS else None
-        if l == 0:
-            widen(1)
+
+            @pl.when((f > 0) & (f < 4))
+            def _():
+                widen(1)
 
         @pl.when(f < 2)
         def _():
-            attend(4 * rows, hook)
+            one_half(l)
 
         @pl.when(f >= 2)
         def _():
-            attend(8 * rows, hook)
+            if l == 0:
+                two_halves_first(l)
+            else:
+                two_halves_second(l)
 
         proj = jnp.dot(att[...], wo[l], preferred_element_type=jnp.float32)
         x = (xs[...] + proj).astype(jnp.bfloat16)
@@ -301,6 +333,9 @@
             pltpu.VMEM((rows, HEADS * PAD), bf),
             pltpu.VMEM((8 * rows, 2 * HEADS * PAD), bf),
             pltpu.VMEM((rows, HEADS * PAD), bf),
+            pltpu.VMEM((rows, HEADS * PAD), jnp.float32),
+            pltpu.VMEM((HEADS, rows, 1), jnp.float32),
+            pltpu.VMEM((HEADS, rows, 1), jnp.float32),
             pltpu.SemaphoreType.DMA((LAYERS,)),
             pltpu.SemaphoreType.DMA((LAYERS, HEADS)),
             pltpu.SemaphoreType.DMA((LAYERS, 2, 5, CHUNKS)),

time: 66.8 us -> 56.5 us (0.85)
  Pallas kernels: 65 us -> 54.1 us
    pallas_call x1, Pallas kernels: 65 us -> 54.1 us  [shards(): pl.pallas_call(functools.partial(kernel, nf), out_shape=jax.ShapeDtypeStr...]
where the time goes in v2:
time: 56.5 us; the launch traced here: 55.8 us
  Pallas kernels  54.1 us (96%)
  local copies, waits for them, and re-layouts  1.61 us (3%)
    pallas_call x1, Pallas kernels, shards(): pl.pallas_call(functools.partial(kernel, nf), out_shape=jax.ShapeDtypeStr...  54.1 us
    unnamed x1, local copies, waits for them, and re-layouts  1.61 us

profile of v2, /device:TPU:27, one launch (start us, length us, event | category | flops | bytes accessed | tf_op | source)
XLA Modules:
  0.0 55.8 jit_solution(14394711128526540241)
XLA Ops:
  0.0 54.1 %shard_map.46 = bf16[1,144,640]{2,1,0:T(8,128)(2,1)} custom-call(bf16[1,144,640]{2,1,0:T(8,128)(2,1)} %tok.1, f32[2,640]{1,0:T(2,128)} %gain.1, bf16[2,640,1920]{2,1,0:T(8,128)(2,1)} %wqkv_hbm.1, bf16[2,640,640]{2,1,0:T(8,128)(2,1)} %wout_hbm.1), custom_call_target="tpu_custom_call" | custom-call | tf_op jit(solution)/shard_map/pallas_call | solution.py:321
  54.1 1.6 %copy.6 = bf16[1,144,640]{2,1,0:T(8,128)(2,1)} copy(bf16[1,144,640]{2,1,0:T(8,128)(2,1)} %shard_map.46) | data formatting | bytes 368640

commit v3 on v2

--- a/solution.py
+++ b/solution.py
@@ -218,10 +218,16 @@
             first_step(l, c)
             prev_step(l, c)
 
+    def leaf_step(l, c):
+        @pl.when((f >= 4) & (f + 2 >= nf))
+        def _():
+            first_step(l, c)
+
     def two_halves_first(l):
         relay(l, 1)
         mate_landed(l, 1)
-        keys_values(l, 1)
+        keys_values(l, 1, [functools.partial(leaf_step, l, c) for c in range(2)])
+        leaf_step(l, 2)
         attend(1, "first", functools.partial(relay, l, 0))
         mate_landed(l, 0)
         keys_values(l, 0)
@@ -284,6 +290,9 @@
             @pl.when(f >= 4)
             def _():
                 prev_steps(l)
+
+            @pl.when((f >= 4) & (f + 2 < nf))
+            def _():
                 first_steps(l)
 
             @pl.when((f > 0) & (f < 4))

time: 56.5 us -> 56.8 us (level)
  no operation moved by 1% of the time
where the time goes in v3:
time: 56.8 us; the launch traced here: 56.1 us
  Pallas kernels  54.4 us (96%)
  local copies, waits for them, and re-layouts  1.61 us (3%)
    pallas_call x1, Pallas kernels, shards(): pl.pallas_call(functools.partial(kernel, nf), out_shape=jax.ShapeDtypeStr...  54.4 us
    unnamed x1, local copies, waits for them, and re-layouts  1.61 us

profile of v3, /device:TPU:27, one launch (start us, length us, event | category | flops | bytes accessed | tf_op | source)
XLA Modules:
  0.0 56.1 jit_solution(771263055815090110)
XLA Ops:
  0.0 54.4 %shard_map.46 = bf16[1,144,640]{2,1,0:T(8,128)(2,1)} custom-call(bf16[1,144,640]{2,1,0:T(8,128)(2,1)} %tok.1, f32[2,640]{1,0:T(2,128)} %gain.1, bf16[2,640,1920]{2,1,0:T(8,128)(2,1)} %wqkv_hbm.1, bf16[2,640,640]{2,1,0:T(8,128)(2,1)} %wout_hbm.1), custom_call_target="tpu_custom_call" | custom-call | tf_op jit(solution)/shard_map/pallas_call | solution.py:330
  54.4 1.6 %copy.6 = bf16[1,144,640]{2,1,0:T(8,128)(2,1)} copy(bf16[1,144,640]{2,1,0:T(8,128)(2,1)} %shard_map.46) | data formatting | bytes 368640
